TPU v7x, 512 devices: a whole 4x8x8 slice. The times are simulated.
512 devices in a mesh: row: 16 (over x_hi, z), col: 32 (over x_lo, y, core).
Axes of the slice: x: 4 (x_hi: 2, x_lo: 2; x = x_hi * 2 + x_lo), y: 8, z: 8, core: 2. Of those that a mesh axis runs over, the one named last changes fastest.
Arguments:
- slots: bfloat16 [3072, 128, 128], P(('row', 'col')), may hold values from -6 to 6
- block_list: int32 [3072], P(('row', 'col')), may hold values from -1 to 15, as said below
- metric: bfloat16 [8192, 4096], P('row', 'col'), may hold values from -0.125 to 0.125
Outputs:
- contracted: float32 [16384, 4096], P('row', 'col')
Inputs may be any that keep to these rules, and one draw needn't show every extreme that they name: `block_list`: the live entries of one device's 6 slots come first and name distinct blocks; -1 marks an unused slot; every device has at least 3 live slots and some device has all 6 live.
All inputs are finite; a program needn't handle non-finite values.
Results may differ from a plain program's by a relative error of at most 0.0003.
Values may be sent and summed in bfloat16 or wider, within the bound.
No kernel may reach another device: no remote copies, remote signals or barrier semaphores. Data moves between devices by JAX's collectives and lax.ppermute only.
A program may use at most 128 MiB of HBM per device.

v0:
```python
import jax
import jax.numpy as jnp
from jax import lax
from jax.sharding import PartitionSpec as P

BLK = 128
PAIR_DEV = 1024


def sent_to_all(shard, axis):
    copies = jnp.broadcast_to(shard, (lax.axis_size(axis), *shard.shape))
    return lax.all_to_all(copies, axis, split_axis=0, concat_axis=0, tiled=True)


def laid_out(tiles, dim):
    tiles = jnp.moveaxis(tiles, 0, dim)
    dims = tiles.shape
    return tiles.reshape(*dims[:dim], dims[dim] * dims[dim + 1], *dims[dim + 2 :])


def gathered_copies(shard, axis, dim):
    tiles = sent_to_all(shard, axis)
    return laid_out(tiles, dim)


def on_device(slots, block_list, metric):
    slot_count = block_list.shape[0]
    width = slots.shape[1]
    out_cols = metric.shape[1]
    metric_band = gathered_copies(metric, "row", 0)
    band_blocks = metric_band.shape[0] // width
    col_blocks = band_blocks // lax.axis_size("col")
    pair_blocks = PAIR_DEV // BLK
    metric_blocks = metric_band.reshape(band_blocks, width, out_cols)
    piece_slots = lax.all_gather(slots, "col", axis=0, tiled=True)
    piece_list = lax.all_gather(block_list, "col", axis=0, tiled=True)
    number = piece_list.shape[0]
    shard_of = jnp.arange(number, dtype=jnp.int32) // slot_count
    is_live = piece_list >= 0
    clipped = jnp.maximum(piece_list, 0)
    pair_block = clipped // col_blocks
    global_block = shard_of * col_blocks + clipped % col_blocks
    rows = metric_blocks[global_block]
    prod = jnp.einsum("sab,sbq->saq", piece_slots, rows, preferred_element_type=jnp.float32)
    placing = ((pair_block[:, None] == jnp.arange(pair_blocks)[None, :]) & is_live[:, None]).astype(
        jnp.float32
    )
    added = jnp.einsum("sp,saq->paq", placing, prod, precision=lax.Precision.HIGHEST)
    return added.reshape(pair_blocks * width, out_cols)


def solution(mesh):
    return jax.shard_map(
        on_device,
        mesh=mesh,
        in_specs=(P(("row", "col"), None, None), P(("row", "col")), P("row", "col")),
        out_specs=P("row", "col"),
        check_vma=False,
    )
```

profile of v0, /device:TPU:133, one launch (start us, length us, event | category | flops | bytes accessed | tf_op | source)
XLA Modules:
  0.0 136.9 jit_solution(17358989224031301215)
XLA Ops:
  6.5 0.0 copy-start
  6.5 0.0 all-gather.2.cloned.1.call-start
  6.5 0.7 all-gather.2.cloned.1.call-update
  7.3 2.6 %broadcast_in_dim.4 = bf16[16,512,128]{2,1,0:T(8,128)(2,1)} broadcast(bf16[512,128]{1,0:T(8,128)(2,1)} %param.5), dimensions={1,2} | broadcast | bytes 2228224 | tf_op jit(solution)/shard_map/broadcast_in_dim | solution.py:11
  9.9 10.9 %all-to-all-start = ((bf16[16,512,128]{2,1,0:T(8,128)(2,1)}), bf16[16,512,128]{2,1,0:T(8,128)(2,1)S(1)}, u32[]{:S(2)}, u32[]{:S(2)}) async-start(bf16[16,512,128]{2,1,0:T(8,128)(2,1)} %broadcast_in_dim.4), calls=%async_computation | async-start | bytes 4194304 | tf_op jit(solution)/shard_map/all_to_all | solution.py:12
  20.8 1.3 dynamic-slice
  22.7 0.0 copy-done
  22.8 0.2 dynamic-update-slice
  23.0 14.8 %all-reduce = s32[192]{0:T(256)S(1)} all-reduce(s32[192]{0:T(256)S(1)} %dynamic-update-slice), channel_id=1, replica_groups=mesh['row'=16,'col'=32] {'col'}, use_global_device_ids=true, to_apply=%add | all-reduce | flops 192 | bytes 1536
  37.8 29.6 %all-to-all-done = bf16[16,512,128]{2,1,0:T(8,128)(2,1)S(1)} async-done(((bf16[16,512,128]{2,1,0:T(8,128)(2,1)}), bf16[16,512,128]{2,1,0:T(8,128)(2,1)S(1)}, u32[]{:S(2)}, u32[]{:S(2)}) %all-to-all-start) | async-done | bytes 2097184 | tf_op jit(solution)/shard_map/all_to_all | solution.py:12
  67.5 8.1 %gather_fusion = bf16[192,128,128]{2,1,0:T(8,128)(2,1)} fusion(bf16[64,128,128]{2,1,0:T(8,128)(2,1)S(1)} %bitcast.11, s32[1024]{0:T(1024)S(1)} %pad_clamp_fusion), kind=kCustom, calls=%fused_computation | custom fusion | bytes 12583680 | tf_op jit(solution)/shard_map/gather | solution.py:43
  75.5 20.3 %all-gather.2.cloned.1.call-done = bf16[192,128,128]{2,1,0:T(8,128)(2,1)} async-done(((bf16[6,128,128]{2,1,0:T(8,128)(2,1)}), bf16[192,128,128]{2,1,0:T(8,128)(2,1)}) %all-gather.2.cloned.1.call-update) | async-done | bytes 6291472 | tf_op jit(solution)/shard_map/all_gather | solution.py:35
  95.8 13.7 %convolution_bitcast_fusion = f32[192,128,128]{1,2,0:T(8,128)} fusion(bf16[192,128,128]{2,1,0:T(8,128)(2,1)} %gather_fusion, bf16[192,128,128]{2,1,0:T(8,128)(2,1)} %all-gather.2.cloned.1.call-done), kind=kOutput, calls=%fused_computation.1 | convolution fusion | flops 805306368 | bytes 25165824 | tf_op jit(solution)/shard_map/sab,sbq->saq/dot_general | solution.py:44
  109.5 12.7 %copy.8 = f32[192,128,128]{2,0,1:T(8,128)} copy(f32[192,128,128]{1,2,0:T(8,128)} %convolution_bitcast_fusion) | data formatting | bytes 25165824 | tf_op jit(solution)/shard_map/sab,sbq->saq/dot_general | solution.py:44
  122.3 6.9 %fusion.2 = f32[8,128,128]{2,0,1:T(8,128)S(1)} fusion(f32[192,128,128]{2,0,1:T(8,128)} %copy.8, s32[192]{0:T(256)S(1)} %get-tuple-element.5, pred[192]{0:T(512)(128)(4,1)S(1)} %broadcast_compare_fusion), kind=kOutput, calls=%fused_computation.5 | convolution fusion | flops 301992960 | bytes 13108160 | tf_op jit(solution)/shard_map/sp,saq->paq/dot_general | solution.py:48
  129.2 0.9 copy.9
  (4 shorter events, 0.0 us)
Async XLA Ops:
  6.5 16.2 %copy-start = (s32[6]{0:T(128)S(1)}, s32[6]{0:T(128)}, u32[]{:S(2)}) copy-start(s32[6]{0:T(128)} %param.4) | copy-start | bytes 76
  6.5 89.3 %all-gather.2.cloned.1.call-start = ((), (), s32[]{:S(2)}) async-start(), calls=%async_computation.1 | async-start | bytes 6488064 | tf_op jit(solution)/shard_map/all_gather | solution.py:35
  9.9 57.6 %all-to-all-start = ((bf16[16,512,128]{2,1,0:T(8,128)(2,1)}), bf16[16,512,128]{2,1,0:T(8,128)(2,1)S(1)}, u32[]{:S(2)}, u32[]{:S(2)}) async-start(bf16[16,512,128]{2,1,0:T(8,128)(2,1)} %broadcast_in_dim.4), calls=%async_computation | async-start | bytes 4194304 | tf_op jit(solution)/shard_map/all_to_all | solution.py:12
Sparse Core Ops, SparseCore 0:
  9.5 86.3 all-gather.1
where the time goes:
time: 137 us
  waiting for transfers between devices  50.7 us (37%)
  local copies, waits for them, and re-layouts  25.8 us (19%)
  matrix products  20.6 us (15%)
  blocking collectives  14.8 us (11%)
  between operations  14.1 us (10%)
  starting transfers between devices  10.9 us (8%)
    all_to_all x1, waiting for transfers between devices, sent_to_all(): return lax.all_to_all(copies, axis, split_axis=0, concat_axis=0, tiled=True)  29.6 us
    all_gather x1, waiting for transfers between devices, on_device(): piece_slots = lax.all_gather(slots, 'col', axis=0, tiled=True)  20.3 us
    unnamed x1, blocking collectives  14.8 us
    dot_general x1, matrix products, on_device(): jnp.einsum('sab,sbq->saq', piece_slots, rows, preferred_element_type=jnp....  13.7 us
    dot_general x1, local copies, waits for them, and re-layouts, on_device(): jnp.einsum('sab,sbq->saq', piece_slots, rows, preferred_element_type=jnp....  12.7 us
    all_to_all x1, starting transfers between devices, sent_to_all(): return lax.all_to_all(copies, axis, split_axis=0, concat_axis=0, tiled=True)  10.9 us
    gather x1, local copies, waits for them, and re-layouts, on_device(): rows = metric_blocks[global_block]  8.05 us
    dot_general x1, matrix products, on_device(): jnp.einsum('sp,saq->paq', placing, prod, precision=lax.Precision.HIGHEST)  6.92 us
  transfers between devices with their start and end apart: 2, of which 2 were waited for; matrix products, arithmetic and copies ran while one was open for 9% of the time, Pallas kernels for 0%

commit v1 on v0

--- a/solution.py
+++ b/solution.py
@@ -32,7 +32,9 @@
     col_blocks = band_blocks // lax.axis_size("col")
     pair_blocks = PAIR_DEV // BLK
     metric_blocks = metric_band.reshape(band_blocks, width, out_cols)
-    piece_slots = lax.all_gather(slots, "col", axis=0, tiled=True)
+    piece_slots = jnp.concatenate(
+        lax.all_to_all(jnp.stack([slots] * lax.axis_size("col")), "col", 0, 0), axis=0
+    )
     piece_list = lax.all_gather(block_list, "col", axis=0, tiled=True)
     number = piece_list.shape[0]
     shard_of = jnp.arange(number, dtype=jnp.int32) // slot_count

time: 137 us -> 269 us (1.96)
  the two profiles are of different devices: /device:TPU:133 before, /device:TPU:8 now
where the time goes in v1:
time: 269 us
  blocking collectives  211 us (78%)
  local copies, waits for them, and re-layouts  28.7 us (11%)
  matrix products  20.6 us (8%)
  starting transfers between devices  7.91 us (3%)
    unnamed x1, blocking collectives  147 us
    all_to_all x1, blocking collectives, sent_to_all(): return lax.all_to_all(copies, axis, split_axis=0, concat_axis=0, tiled=True)  63.6 us
    dot_general x1, matrix products, on_device(): jnp.einsum('sab,sbq->saq', piece_slots, rows, preferred_element_type=jnp....  13.7 us
    dot_general x1, local copies, waits for them, and re-layouts, on_device(): jnp.einsum('sab,sbq->saq', piece_slots, rows, preferred_element_type=jnp....  12.8 us
    gather x1, local copies, waits for them, and re-layouts, on_device(): rows = metric_blocks[global_block]  8 us
    all_to_all x1, starting transfers between devices, on_device(): lax.all_to_all(jnp.stack([slots] * lax.axis_size('col')), 'col', 0, 0)  7.91 us
    dot_general x1, matrix products, on_device(): jnp.einsum('sp,saq->paq', placing, prod, precision=lax.Precision.HIGHEST)  6.89 us
  transfers between devices with their start and end apart: 1, of which 0 were waited for; matrix products, arithmetic and copies ran while one was open for 4% of the time, Pallas kernels for 0%

profile of v1, /device:TPU:8, one launch (start us, length us, event | category | flops | bytes accessed | tf_op | source)
XLA Modules:
  0.0 268.8 jit_solution(3402161775482614505)
XLA Ops:
  0.0 0.0 copy-start
  0.0 1.3 broadcast_in_dim.4
  1.4 63.6 %all_to_all.10 = bf16[16,512,128]{2,1,0:T(8,128)(2,1)S(1)} all-to-all(bf16[16,512,128]{2,1,0:T(8,128)(2,1)S(1)} %broadcast_in_dim.4), channel_id=1, replica_groups=mesh['row'=16,'col'=32] {'row'}, dimensions={0} | all-to-all | bytes 4194304 | tf_op jit(solution)/shard_map/all_to_all | solution.py:12
  64.9 0.0 copy-done
  64.9 4.2 %stack.2 = bf16[32,6,128,128]{3,2,1,0:T(8,128)(2,1)} broadcast(bf16[6,128,128]{2,1,0:T(8,128)(2,1)S(1)} %copy-done), dimensions={1,2,3} | broadcast | bytes 6488064 | tf_op jit(solution)/shard_map/stack | solution.py:36
  69.1 0.0 copy-start.1
  69.1 7.9 %all-to-all-start.1 = ((bf16[32,6,128,128]{3,2,1,0:T(8,128)(2,1)}), bf16[32,6,128,128]{3,2,1,0:T(8,128)(2,1)}, u32[]{:S(2)}, u32[]{:S(2)}) async-start(bf16[32,6,128,128]{3,2,1,0:T(8,128)(2,1)} %stack.2), calls=%async_computation.1 | async-start | bytes 12582912 | tf_op jit(solution)/shard_map/all_to_all | solution.py:36
  77.1 1.3 dynamic-slice
  79.0 0.0 copy-done.1
  79.0 0.2 dynamic-update-slice
  79.2 147.3 %all-reduce = s32[192]{0:T(256)S(1)} all-reduce(s32[192]{0:T(256)S(1)} %dynamic-update-slice), channel_id=1, replica_groups=mesh['row'=16,'col'=32] {'col'}, use_global_device_ids=true, to_apply=%add | all-reduce | flops 192 | bytes 1536
  226.6 8.0 %gather_fusion = bf16[192,128,128]{2,1,0:T(8,128)(2,1)} fusion(bf16[64,128,128]{2,1,0:T(8,128)(2,1)S(1)} %bitcast.12, s32[1024]{0:T(1024)S(1)} %pad_clamp_fusion), kind=kCustom, calls=%fused_computation | custom fusion | bytes 12583680 | tf_op jit(solution)/shard_map/gather | solution.py:45
  234.6 0.0 all-to-all-done.1
  234.6 13.7 %fusion.9 = f32[192,128,128]{2,1,0:T(8,128)} fusion(bf16[192,128,128]{2,1,0:T(8,128)(2,1)} %gather_fusion, bf16[192,128,128]{2,1,0:T(8,128)(2,1)} %bitcast.3), kind=kOutput, calls=%fused_computation.20 | convolution fusion | flops 805306368 | bytes 25165824 | tf_op jit(solution)/shard_map/sab,sbq->saq/dot_general | solution.py:46
  248.3 12.8 %copy.5 = f32[192,128,128]{1,0,2:T(8,128)} copy(f32[192,128,128]{2,1,0:T(8,128)} %fusion.9) | data formatting | bytes 25165824 | tf_op jit(solution)/shard_map/sab,sbq->saq/dot_general | solution.py:46
  261.0 6.9 %fusion = f32[8,128,128]{2,0,1:T(8,128)S(1)} fusion(f32[192,128,128]{1,0,2:T(8,128)} %copy.5, s32[192]{0:T(256)S(1)} %get-tuple-element.5, pred[192]{0:T(512)(128)(4,1)S(1)} %broadcast_compare_fusion), kind=kOutput, calls=%fused_computation.1 | convolution fusion | flops 301992960 | bytes 13108160 | tf_op jit(solution)/shard_map/sp,saq->paq/dot_general | solution.py:50
  267.9 0.9 copy.4
  (4 shorter events, 0.0 us)
Async XLA Ops:
  0.0 64.9 %copy-start = (bf16[6,128,128]{2,1,0:T(8,128)(2,1)S(1)}, bf16[6,128,128]{2,1,0:T(8,128)(2,1)}, u32[]{:S(2)}) copy-start(bf16[6,128,128]{2,1,0:T(8,128)(2,1)} %param.3) | copy-start | bytes 589828
  69.1 9.9 %copy-start.1 = (s32[6]{0:T(128)S(1)}, s32[6]{0:T(128)}, u32[]{:S(2)}) copy-start(s32[6]{0:T(128)} %param.4) | copy-start | bytes 76
  69.1 165.4 %all-to-all-start.1 = ((bf16[32,6,128,128]{3,2,1,0:T(8,128)(2,1)}), bf16[32,6,128,128]{3,2,1,0:T(8,128)(2,1)}, u32[]{:S(2)}, u32[]{:S(2)}) async-start(bf16[32,6,128,128]{3,2,1,0:T(8,128)(2,1)} %stack.2), calls=%async_computation.1 | async-start | bytes 12582912 | tf_op jit(solution)/shard_map/all_to_all | solution.py:36
